TPU v7x, 32 devices: a whole 2x2x4 slice. The times are simulated.
32 devices in a mesh: grp: 4 (over y, x), shard: 8 (over z, core).
Axes of the slice: x: 2, y: 2, z: 4, core: 2. Of those that a mesh axis runs over, the one named last changes fastest.
Arguments:
- partials: bfloat16 [4, 1536, 2, 4096], P('grp', 'shard'), may hold values from -225 to 225
- weights: float32 [1536, 2, 4096], P('shard'), may hold values from -4 to 4
- subspace: bfloat16 [1536, 2, 256], P('shard'), may hold values from -6 to 6
- moment_one: float32 [4096, 2, 256], P('shard'), may hold values from -2 to 2
- moment_two: float32 [4096, 2, 256], P('shard'), may hold values from 0.001 to 0.1
Outputs:
- new_weights: float32 [1536, 2, 4096], P('shard')
- new_moment_one: float32 [4096, 2, 256], P('shard')
- new_moment_two: float32 [4096, 2, 256], P('shard')
- new_subspace: bfloat16 [1536, 2, 256], P('shard')
All inputs are finite; a program needn't handle non-finite values.
Results may differ from a plain program's by a relative error of at most 0.01.
Values may be sent and summed in bfloat16 or wider, within the bound.
No kernel may reach another device: no remote copies, remote signals or barrier semaphores. Data moves between devices by JAX's collectives and lax.ppermute only.
A program may use at most 128 MiB of HBM per device.

v0:
```python
import math
import jax
import jax.numpy as jnp
from jax import lax
from jax.sharding import PartitionSpec as P

D = 1536
first_fix = 1.0 - 0.9**10
second_fix = 1.0 - 0.999**10


def per_device(partials, weights, subspace, moment_one, moment_two):
    gradient = lax.psum(partials[0].astype(jnp.float32).astype(jnp.bfloat16), "grp")
    inv_root = 1.0 / math.sqrt(D)
    column_block = gradient
    projected = lax.psum_scatter(
        jnp.einsum("dmf,dmk->fmk", column_block, subspace, preferred_element_type=jnp.float32)
        * inv_root,
        "shard",
        scatter_dimension=0,
        tiled=True,
    )
    new_moment_one = 0.9 * moment_one + 0.1 * projected
    new_moment_two = 0.999 * moment_two + 0.001 * projected * projected
    direction = (
        new_moment_one / first_fix / (jnp.sqrt(new_moment_two / second_fix) + 1e-08)
    ).astype(jnp.bfloat16)
    projected_half = projected.astype(jnp.bfloat16)
    update = jnp.einsum(
        "dmk,fmk->dmf",
        subspace,
        lax.all_gather(direction, "shard", axis=0, tiled=True),
        preferred_element_type=jnp.float32,
    )
    increment = update
    column_block = gradient
    spanned = jnp.einsum(
        "dmf,fmk->dmk",
        column_block,
        lax.all_gather(projected_half, "shard", axis=0, tiled=True),
        preferred_element_type=jnp.float32,
    )
    increment, spanned = (increment, spanned)
    new_weights = weights - increment * inv_root
    local_gram = jnp.einsum("dmk,dml->mkl", spanned, spanned, precision=lax.Precision.HIGHEST)
    gram_matrix = lax.psum(local_gram, "shard")
    normalizer = 1.7 / jnp.sqrt(jnp.sqrt(jnp.sum(gram_matrix * gram_matrix, axis=(1, 2))) + 1e-06)
    oriented = spanned * normalizer[None, :, None]
    own_gram = jnp.einsum("dmk,dml->mkl", oriented, oriented, precision=lax.Precision.HIGHEST)
    ortho_gram = lax.psum(own_gram, "shard")
    polished = 1.5 * oriented - 0.5 * jnp.einsum(
        "dmk,mkl->dml", oriented, ortho_gram, precision=lax.Precision.HIGHEST
    )
    new_subspace = (math.sqrt(D) * polished).astype(jnp.bfloat16)
    return (new_weights, new_moment_one, new_moment_two, new_subspace)


def solution(mesh):
    return jax.shard_map(
        per_device,
        mesh=mesh,
        in_specs=(
            P("grp", "shard", None, None),
            P("shard", None, None),
            P("shard", None, None),
            P("shard", None, None),
            P("shard", None, None),
        ),
        out_specs=(
            P("shard", None, None),
            P("shard", None, None),
            P("shard", None, None),
            P("shard", None, None),
        ),
        check_vma=False,
    )
```

profile of v0, /device:TPU:0, one launch (start us, length us, event | category | flops | bytes accessed | tf_op | source)
XLA Modules:
  0.0 424.1 jit_solution(8756850632732030668)
XLA Ops:
  7.2 5.7 %copy.29 = bf16[1,192,2,4096]{3,1,2,0:T(8,128)(2,1)} copy(bf16[1,192,2,4096]{3,2,1,0:T(2,128)(2,1)} %param.5) | data formatting | bytes 6291456 | tf_op args[0]
  13.0 90.0 %all-reduce.4.cloned.1.call-done = bf16[192,2,4096]{2,0,1:T(8,128)(2,1)} async-done(((bf16[192,2,4096]{2,0,1:T(8,128)(2,1)}), bf16[192,2,4096]{2,0,1:T(8,128)(2,1)}) %all-reduce.4.cloned.1.call-update) | async-done | bytes 3145744 | tf_op jit(solution)/shard_map/psum | solution.py:13
  103.0 6.5 %multiply_bitcast_fusion = f32[4096,2,256]{0,2,1:T(8,128)} fusion(bf16[192,2,4096]{2,0,1:T(8,128)(2,1)} %all-reduce.4.cloned.1.call-done, bf16[192,2,256]{2,1,0:T(2,128)(2,1)S(1)} %copy-done.3), kind=kOutput, calls=%fused_computation | convolution fusion | flops 807403520 | bytes 11730944 | tf_op jit(solution)/shard_map/dmf,dmk->fmk/dot_general | solution.py:17
  109.6 1.1 copy-done.2
  110.7 1.6 copy.9
  112.3 2.4 copy.12
  114.7 84.6 %reduce-scatter.2.cloned.1.call-done = f32[512,2,256]{0,2,1:T(8,128)} async-done(((f32[4096,2,256]{0,2,1:T(8,128)}), f32[512,2,256]{0,2,1:T(8,128)}) %reduce-scatter.2.cloned.1.call-update) | async-done | bytes 1048592 | tf_op jit(solution)/shard_map/reduce_scatter | solution.py:16
  199.3 4.4 %divide_convert_fusion = (bf16[512,2,256]{0,2,1:T(8,128)(2,1)}, f32[512,2,256]{0,2,1:T(8,128)}, f32[512,2,256]{0,2,1:T(8,128)}, bf16[512,2,256]{0,2,1:T(8,128)(2,1)}) fusion(f32[512,2,256]{0,2,1:T(8,128)} %reduce-scatter.2.cloned.1.call-done, f32[512,2,256]{0,2,1:T(8,128)} %copy.9, f32[512,2,256]{0,2,1:T(8,128)} %copy.12), kind=kLoop, calls=%fused_computation.11 | loop fusion | flops 3407872 | bytes 6291456 | tf_op jit(solution)/shard_map/convert_element_type | solution.py:27
  203.7 0.0 all-reduce.6.cloned.1.call-start
  203.8 45.6 %all-gather.5.cloned.1.call-done = bf16[4096,2,256]{0,2,1:T(8,128)(2,1)} async-done(((bf16[512,2,256]{0,2,1:T(8,128)(2,1)}), bf16[4096,2,256]{0,2,1:T(8,128)(2,1)}) %all-gather.5.cloned.1.call-update) | async-done | bytes 4194320 | tf_op jit(solution)/shard_map/all_gather | solution.py:40
  249.4 3.7 convolution_bitcast_fusion
  253.1 1.9 fusion.13
  255.1 0.5 all-gather.3.cloned.1.call-update
  255.7 2.4 copy.18
  258.1 1.3 copy.19
  259.4 50.6 %all-reduce.6.cloned.1.call-done = f32[2,256,256]{2,1,0:T(8,128)} async-done(((f32[2,256,256]{2,1,0:T(8,128)}), f32[2,256,256]{2,1,0:T(8,128)}) %all-reduce.6.cloned.1.call-update) | async-done | bytes 524304 | tf_op jit(solution)/shard_map/psum | solution.py:46
  310.1 1.2 multiply_reduce_fusion
  311.3 2.0 fusion.5
  313.3 44.4 %all-gather.3.cloned.1.call-done = bf16[4096,2,256]{0,2,1:T(8,128)(2,1)} async-done(((bf16[512,2,256]{0,2,1:T(8,128)(2,1)}), bf16[4096,2,256]{0,2,1:T(8,128)(2,1)}) %all-gather.3.cloned.1.call-update) | async-done | bytes 4194320 | tf_op jit(solution)/shard_map/all_gather | solution.py:32
  357.7 8.7 %bitcast_subtract_fusion = f32[192,2,4096]{2,0,1:T(8,128)S(1)} fusion(f32[192,2,4096]{2,1,0:T(2,128)} %param.6, bf16[4096,2,256]{0,2,1:T(8,128)(2,1)} %all-gather.3.cloned.1.call-done, bf16[192,2,256]{2,1,0:T(2,128)(2,1)} %param.7), kind=kOutput, calls=%fused_computation.1 | convolution fusion | flops 808452096 | bytes 16973824 | tf_op jit(solution)/shard_map/dmk,fmk->dmf/dot_general | solution.py:29
  366.4 7.6 %copy.17 = f32[192,2,4096]{2,1,0:T(2,128)} copy(f32[192,2,4096]{2,0,1:T(8,128)S(1)} %bitcast_subtract_fusion) | data formatting | bytes 12582912
  374.0 40.8 %all-reduce.8.cloned.1.call-done = f32[2,256,256]{2,1,0:T(8,128)} async-done(((f32[2,256,256]{2,1,0:T(8,128)}), f32[2,256,256]{2,1,0:T(8,128)}) %all-reduce.8.cloned.1.call-update) | async-done | bytes 524304 | tf_op jit(solution)/shard_map/psum | solution.py:50
  414.8 1.6 fusion.3
  416.4 0.9 copy.20
  (18 shorter events, 0.3 us)
Async XLA Ops:
  7.2 95.8 %copy-start.3 = (bf16[192,2,256]{2,1,0:T(2,128)(2,1)S(1)}, bf16[192,2,256]{2,1,0:T(2,128)(2,1)}, u32[]{:S(2)}) copy-start(bf16[192,2,256]{2,1,0:T(2,128)(2,1)} %param.7) | copy-start | bytes 589828
  7.2 95.8 %all-reduce.4.cloned.1.call-start = ((), (), s32[]{:S(2)}) async-start(), calls=%async_computation.1 | async-start | bytes 6291456 | tf_op jit(solution)/shard_map/psum | solution.py:13
  12.9 186.4 %reduce-scatter.2.cloned.1.call-start = ((), (), s32[]{:S(2)}) async-start(), calls=%async_computation.2 | async-start | bytes 9437184 | tf_op jit(solution)/shard_map/reduce_scatter | solution.py:16
  109.5 1.2 copy-start.2
  109.5 139.8 %all-gather.5.cloned.1.call-start = ((), (), s32[]{:S(2)}) async-start(), calls=%async_computation.4 | async-start | bytes 4718592 | tf_op jit(solution)/shard_map/all_gather | solution.py:40
  112.3 137.1 %copy-start = (bf16[192,2,4096]{2,0,1:T(8,128)(2,1)S(1)}, bf16[192,2,4096]{2,0,1:T(8,128)(2,1)}, u32[]{:S(2)}) copy-start(bf16[192,2,4096]{2,0,1:T(8,128)(2,1)} %all-reduce.4.cloned.1.call-done) | copy-start | bytes 9437188
  203.7 106.3 %all-reduce.6.cloned.1.call-start = ((), (), s32[]{:S(2)}) async-start(), calls=%async_computation.5 | async-start | bytes 1048576 | tf_op jit(solution)/shard_map/psum | solution.py:46
  253.1 5.0 %copy-start.1 = (f32[512,2,256]{0,2,1:T(8,128)S(1)}, f32[512,2,256]{0,2,1:T(8,128)}, u32[]{:S(2)}) copy-start(f32[512,2,256]{0,2,1:T(8,128)} %get-tuple-element.10) | copy-start | bytes 3145732
  255.1 102.6 %all-gather.3.cloned.1.call-start = ((), (), s32[]{:S(2)}) async-start(), calls=%async_computation.3 | async-start | bytes 4718592 | tf_op jit(solution)/shard_map/all_gather | solution.py:32
  255.7 159.1 %all-reduce.8.cloned.1.call-start = ((), (), s32[]{:S(2)}) async-start(), calls=%async_computation.6 | async-start | bytes 1048576 | tf_op jit(solution)/shard_map/psum | solution.py:50
Sparse Core Ops, SparseCore 0:
  13.1 89.8 all-reduce.3
  109.7 89.5 reduce-scatter.1
  203.8 45.5 all-gather.4
  255.2 54.8 all-reduce.5
  311.5 46.1 all-gather.2
  359.9 54.8 all-reduce.7
where the time goes:
time: 424 us
  waiting for transfers between devices  357 us (84%)
  matrix products  24.5 us (6%)
  local copies, waits for them, and re-layouts  23 us (5%)
  between operations  14.2 us (3%)
  other arithmetic  5.61 us (1%)
    psum x1, waiting for transfers between devices, per_device(): lax.psum(partials[0].astype(jnp.float32).astype(jnp.bfloat16), 'grp')  90 us
    reduce_scatter x1, waiting for transfers between devices, per_device(): lax.psum_scatter(jnp.einsum('dmf,dmk->fmk', column_block, subspace, prefe...  84.6 us
    psum x1, waiting for transfers between devices, per_device(): gram_matrix = lax.psum(local_gram, 'shard')  50.6 us
    all_gather x1, waiting for transfers between devices, per_device(): lax.all_gather(projected_half, 'shard', axis=0, tiled=True)  45.6 us
    all_gather x1, waiting for transfers between devices, per_device(): lax.all_gather(direction, 'shard', axis=0, tiled=True)  44.4 us
    psum x1, waiting for transfers between devices, per_device(): ortho_gram = lax.psum(own_gram, 'shard')  40.8 us
    unnamed x15, local copies, waits for them, and re-layouts  23 us
    dot_general x1, matrix products, per_device(): jnp.einsum('dmk,fmk->dmf', subspace, lax.all_gather(direction, 'shard', a...  8.71 us
  transfers between devices with their start and end apart: 6, of which 6 were waited for; matrix products, arithmetic and copies ran while one was open for 6% of the time, Pallas kernels for 0%

commit v1 on v0

--- a/solution.py
+++ b/solution.py
@@ -7,6 +7,28 @@
 D = 1536
 first_fix = 1.0 - 0.9**10
 second_fix = 1.0 - 0.999**10
+
+
+def laid_out(parts, dim):
+    dims = list(parts.shape[1:])
+    dims[dim] *= parts.shape[0]
+    return jnp.moveaxis(parts, 0, dim).reshape(dims)
+
+
+def collect(value, axis, dim):
+    size = lax.axis_size(axis)
+    pairs = [(i, (i + 1) % size) for i in range(size)]
+    back = [(b, a) for a, b in pairs]
+    lower, upper = ([], [])
+    for step in range(size - 1):
+        if step % 2 == 0:
+            lower.append(lax.ppermute(lower[-1] if lower else value, axis, pairs))
+        else:
+            upper.append(lax.ppermute(upper[-1] if upper else value, axis, back))
+    tiles = jnp.stack([*lower[::-1], value, *upper])
+    shift = lax.axis_index(axis) - len(lower)
+    tiles = tiles[(jnp.arange(size) - shift) % size]
+    return laid_out(tiles, dim)
 
 
 def per_device(partials, weights, subspace, moment_one, moment_two):
@@ -27,10 +49,7 @@
     ).astype(jnp.bfloat16)
     projected_half = projected.astype(jnp.bfloat16)
     update = jnp.einsum(
-        "dmk,fmk->dmf",
-        subspace,
-        lax.all_gather(direction, "shard", axis=0, tiled=True),
-        preferred_element_type=jnp.float32,
+        "dmk,fmk->dmf", subspace, collect(direction, "shard", 0), preferred_element_type=jnp.float32
     )
     increment = update
     column_block = gradient

time: 424 us -> 423 us (level)
  waiting for transfers between devices: 357 us -> 320 us
  local copies, waits for them, and re-layouts: 23 us -> 47.9 us
  starting transfers between devices: 0.24 us -> 10.9 us
    ppermute x0 -> x7, waiting for transfers between devices: none -> 57.2 us  [the longest x4 57.2 us: collect(): lower.append(lax.ppermute(lower[-1] if lower else value, axis, pairs))]
    all_gather x1, waiting for transfers between devices: 45.6 us -> 0.01 us  [per_device(): lax.all_gather(projected_half, 'shard', axis=0, tiled=True)]
    all_gather x1 -> x0, waiting for transfers between devices: 44.4 us -> none  [per_device(): lax.all_gather(direction, 'shard', axis=0, tiled=True)]
    unnamed x15 -> x26, local copies, waits for them, and re-layouts: 23 us -> 34.9 us
    gather x0 -> x2, local copies, waits for them, and re-layouts: none -> 11.1 us  [collect(): tiles = tiles[(jnp.arange(size) - shift) % size]]
    ppermute x0 -> x7, starting transfers between devices: none -> 10.7 us  [the longest x3 10.6 us: collect(): upper.append(lax.ppermute(upper[-1] if upper else value, axis, back))]
  transfers between devices with their start and end apart: 6 -> 12, of which waited for: 6 -> 8; matrix products, arithmetic and copies ran while one was open for 6% -> 13% of each run, Pallas kernels for 0% -> 0%
where the time goes in v1:
time: 423 us; the launch traced here: 422 us
  waiting for transfers between devices  320 us (76%)
  local copies, waits for them, and re-layouts  47.9 us (11%)
  matrix products  24.4 us (6%)
  between operations  13.9 us (3%)
  starting transfers between devices  10.9 us (3%)
  other arithmetic  4.86 us (1%)
    psum x1, waiting for transfers between devices, per_device(): lax.psum(partials[0].astype(jnp.float32).astype(jnp.bfloat16), 'grp')  90 us
    reduce_scatter x1, waiting for transfers between devices, per_device(): lax.psum_scatter(jnp.einsum('dmf,dmk->fmk', column_block, subspace, prefe...  86.3 us
    ppermute x4, waiting for transfers between devices, collect(): lower.append(lax.ppermute(lower[-1] if lower else value, axis, pairs))  57.2 us
    psum x1, waiting for transfers between devices, per_device(): gram_matrix = lax.psum(local_gram, 'shard')  47.2 us
    psum x1, waiting for transfers between devices, per_device(): ortho_gram = lax.psum(own_gram, 'shard')  39.1 us
    unnamed x26, local copies, waits for them, and re-layouts  34.9 us
    gather x2, local copies, waits for them, and re-layouts, collect(): tiles = tiles[(jnp.arange(size) - shift) % size]  11.1 us
    ppermute x3, starting transfers between devices, collect(): upper.append(lax.ppermute(upper[-1] if upper else value, axis, back))  10.6 us
  transfers between devices with their start and end apart: 12, of which 8 were waited for; matrix products, arithmetic and copies ran while one was open for 13% of the time, Pallas kernels for 0%

profile of v1, /device:TPU:0, one launch (start us, length us, event | category | flops | bytes accessed | tf_op | source)
XLA Modules:
  0.0 421.7 jit_solution(9758437922620471443)
XLA Ops:
  7.2 5.7 %copy.39 = bf16[1,192,2,4096]{3,1,2,0:T(8,128)(2,1)} copy(bf16[1,192,2,4096]{3,2,1,0:T(2,128)(2,1)} %param.5) | data formatting | bytes 6291456 | tf_op args[0]
  13.0 90.0 %all-reduce.4.cloned.1.call-done = bf16[192,2,4096]{2,0,1:T(8,128)(2,1)} async-done(((bf16[192,2,4096]{2,0,1:T(8,128)(2,1)}), bf16[192,2,4096]{2,0,1:T(8,128)(2,1)}) %all-reduce.4.cloned.1.call-update) | async-done | bytes 3145744 | tf_op jit(solution)/shard_map/psum | solution.py:35
  103.0 6.5 %multiply_bitcast_fusion = f32[4096,2,256]{0,2,1:T(8,128)} fusion(bf16[192,2,4096]{2,0,1:T(8,128)(2,1)} %all-reduce.4.cloned.1.call-done, bf16[192,2,256]{2,1,0:T(2,128)(2,1)S(1)} %copy-done.3), kind=kOutput, calls=%fused_computation.1 | convolution fusion | flops 807403520 | bytes 11730944 | tf_op jit(solution)/shard_map/dmf,dmk->fmk/dot_general | solution.py:39
  113.0 86.3 %reduce-scatter.2.cloned.1.call-done = f32[512,2,256]{0,2,1:T(8,128)} async-done(((f32[4096,2,256]{0,2,1:T(8,128)}), f32[512,2,256]{0,2,1:T(8,128)}) %reduce-scatter.2.cloned.1.call-update) | async-done | bytes 1048592 | tf_op jit(solution)/shard_map/reduce_scatter | solution.py:38
  199.3 3.6 divide_convert_fusion
  203.0 10.8 %collective-permute-done = bf16[512,2,256]{0,2,1:T(8,128)(2,1)S(1)} collective-permute-done((bf16[512,2,256]{0,2,1:T(8,128)(2,1)}, bf16[512,2,256]{0,2,1:T(8,128)(2,1)S(1)}, u32[]{:S(2)}, u32[]{:S(2)}) %collective-permute-start) | collective-permute-done | bytes 524320 | tf_op jit(solution)/shard_map/ppermute | solution.py:25
  214.6 3.5 collective-permute-start.4
  218.2 22.8 %collective-permute-done.1 = bf16[512,2,256]{0,2,1:T(8,128)(2,1)S(1)} collective-permute-done((bf16[512,2,256]{0,2,1:T(8,128)(2,1)S(1)}, bf16[512,2,256]{0,2,1:T(8,128)(2,1)S(1)}, u32[]{:S(2)}, u32[]{:S(2)}) %collective-permute-start.1) | collective-permute-done | bytes 524320 | tf_op jit(solution)/shard_map/ppermute | solution.py:25
  241.8 3.5 collective-permute-start.5
  245.4 20.0 %collective-permute-done.2 = bf16[512,2,256]{0,2,1:T(8,128)(2,1)} collective-permute-done((bf16[512,2,256]{0,2,1:T(8,128)(2,1)S(1)}, bf16[512,2,256]{0,2,1:T(8,128)(2,1)}, u32[]{:S(2)}, u32[]{:S(2)}) %collective-permute-start.2) | collective-permute-done | bytes 524320 | tf_op jit(solution)/shard_map/ppermute | solution.py:25
  266.7 2.4 copy.30
  269.1 3.5 collective-permute-start.6
  272.6 3.6 collective-permute-done.3
  286.4 3.7 convolution_bitcast_fusion
  290.1 1.9 fusion.15
  292.1 1.9 bitcast_dynamic-update-slice_fusion.1
  293.9 1.9 bitcast_dynamic-update-slice_fusion
  295.8 4.9 %gather_fusion = bf16[8,512,2,256]{1,3,2,0:T(8,128)(2,1)} fusion(bf16[8,512,2,256]{1,3,2,0:T(8,128)(2,1)} %bitcast_dynamic-update-slice_fusion, s32[1024]{0:T(1024)S(1)} %pad_clamp_fusion), kind=kCustom, calls=%fused_computation | custom fusion | bytes 8388640 | tf_op jit(solution)/shard_map/gather | solution.py:30
  300.8 6.2 %copy.24 = bf16[8,512,2,256]{3,1,0,2:T(8,128)(2,1)} copy(bf16[8,512,2,256]{1,3,2,0:T(8,128)(2,1)} %gather_fusion) | data formatting | bytes 8388608 | tf_op jit(solution)/shard_map/gather | solution.py:30
  307.0 47.2 %all-reduce.6.cloned.1.call-done = f32[2,256,256]{2,1,0:T(8,128)} async-done(((f32[2,256,256]{2,1,0:T(8,128)}), f32[2,256,256]{2,1,0:T(8,128)}) %all-reduce.6.cloned.1.call-update) | async-done | bytes 524304 | tf_op jit(solution)/shard_map/psum | solution.py:65
  355.4 1.9 fusion.5
  357.3 8.7 %bitcast_subtract_fusion = f32[192,2,4096]{2,0,1:T(8,128)S(1)} fusion(f32[192,2,4096]{2,1,0:T(2,128)} %param.6, bf16[4096,2,256]{2,0,1:T(8,128)(2,1)} %bitcast.43, bf16[192,2,256]{2,1,0:T(2,128)(2,1)} %param.7), kind=kOutput, calls=%fused_computation.2 | convolution fusion | flops 808452096 | bytes 16973824 | tf_op jit(solution)/shard_map/dmk,fmk->dmf/dot_general | solution.py:51
  366.0 7.6 %copy.28 = f32[192,2,4096]{2,1,0:T(2,128)} copy(f32[192,2,4096]{2,0,1:T(8,128)S(1)} %bitcast_subtract_fusion) | data formatting | bytes 12582912
  373.6 39.1 %all-reduce.8.cloned.1.call-done = f32[2,256,256]{2,1,0:T(8,128)} async-done(((f32[2,256,256]{2,1,0:T(8,128)}), f32[2,256,256]{2,1,0:T(8,128)}) %all-reduce.8.cloned.1.call-update) | async-done | bytes 524304 | tf_op jit(solution)/shard_map/psum | solution.py:69
  (45 shorter events, 20.6 us)
Async XLA Ops:
  7.2 95.8 %copy-start.3 = (bf16[192,2,256]{2,1,0:T(2,128)(2,1)S(1)}, bf16[192,2,256]{2,1,0:T(2,128)(2,1)}, u32[]{:S(2)}) copy-start(bf16[192,2,256]{2,1,0:T(2,128)(2,1)} %param.7) | copy-start | bytes 589828
  7.2 95.8 %all-reduce.4.cloned.1.call-start = ((), (), s32[]{:S(2)}) async-start(), calls=%async_computation.1 | async-start | bytes 6291456 | tf_op jit(solution)/shard_map/psum | solution.py:35
  12.9 186.3 %reduce-scatter.2.cloned.1.call-start = ((), (), s32[]{:S(2)}) async-start(), calls=%async_computation.2 | async-start | bytes 9437184 | tf_op jit(solution)/shard_map/reduce_scatter | solution.py:38
  109.5 1.2 copy-start.2
  109.5 176.9 %all-gather.2.cloned.1.call-start = ((), (), s32[]{:S(2)}) async-start(), calls=%async_computation.3 | async-start | bytes 4718592 | tf_op jit(solution)/shard_map/all_gather | solution.py:59
  202.9 151.2 %all-reduce.6.cloned.1.call-start = ((), (), s32[]{:S(2)}) async-start(), calls=%async_computation.4 | async-start | bytes 1048576 | tf_op jit(solution)/shard_map/psum | solution.py:65
  203.0 10.8 %collective-permute-start = (bf16[512,2,256]{0,2,1:T(8,128)(2,1)}, bf16[512,2,256]{0,2,1:T(8,128)(2,1)S(1)}, u32[]{:S(2)}, u32[]{:S(2)}) collective-permute-start(bf16[512,2,256]{0,2,1:T(8,128)(2,1)} %get-tuple-element.12), channel_id=1, source_target_pairs={{0,1},{1,2},{2,3},{3,4},{4,5},{5,6},{6,7},{7,0},{8,9},{9,10},{10,1... | collective-permute-start | bytes 1572872 | tf_op jit(solution)/shard_map/ppermute | solution.py:25
  213.8 0.8 copy-start.4
  214.6 26.4 %collective-permute-start.1 = (bf16[512,2,256]{0,2,1:T(8,128)(2,1)S(1)}, bf16[512,2,256]{0,2,1:T(8,128)(2,1)S(1)}, u32[]{:S(2)}, u32[]{:S(2)}) collective-permute-start(bf16[512,2,256]{0,2,1:T(8,128)(2,1)S(1)} %collective-permute-done), channel_id=1, source_target_pairs={{0,1},{1,2},{2,3},{3,4},{4,5},{5,6},{6,7},{7,0},{8,9},{9,10},{10,1... | collective-permute-start | bytes 1572872 | tf_op jit(solution)/shard_map/ppermute | solution.py:25
  214.6 27.2 %collective-permute-start.4 = (bf16[512,2,256]{0,2,1:T(8,128)(2,1)}, bf16[512,2,256]{0,2,1:T(8,128)(2,1)}, u32[]{:S(2)}, u32[]{:S(2)}) collective-permute-start(bf16[512,2,256]{0,2,1:T(8,128)(2,1)} %get-tuple-element.12), channel_id=1, source_target_pairs={{1,0},{2,1},{3,2},{4,3},{5,4},{6,5},{7,6},{0,7},{9,8},{10,9},{11,1... | collective-permute-start | bytes 1572872 | tf_op jit(solution)/shard_map/ppermute | solution.py:27
  241.0 0.8 copy-start.5
  241.8 23.5 %collective-permute-start.2 = (bf16[512,2,256]{0,2,1:T(8,128)(2,1)S(1)}, bf16[512,2,256]{0,2,1:T(8,128)(2,1)}, u32[]{:S(2)}, u32[]{:S(2)}) collective-permute-start(bf16[512,2,256]{0,2,1:T(8,128)(2,1)S(1)} %collective-permute-done.1), channel_id=1, source_target_pairs={{0,1},{1,2},{2,3},{3,4},{4,5},{5,6},{6,7},{7,0},{8,9},{9,10},{10,1... | collective-permute-start | bytes 1572872 | tf_op jit(solution)/shard_map/ppermute | solution.py:25
  241.8 27.3 %collective-permute-start.5 = (bf16[512,2,256]{0,2,1:T(8,128)(2,1)}, bf16[512,2,256]{0,2,1:T(8,128)(2,1)}, u32[]{:S(2)}, u32[]{:S(2)}) collective-permute-start(bf16[512,2,256]{0,2,1:T(8,128)(2,1)} %collective-permute-done.4), channel_id=1, source_target_pairs={{1,0},{2,1},{3,2},{4,3},{5,4},{6,5},{7,6},{0,7},{9,8},{10,9},{11,1... | collective-permute-start | bytes 1572872 | tf_op jit(solution)/shard_map/ppermute | solution.py:27
  265.4 10.9 %collective-permute-start.3 = (bf16[512,2,256]{0,2,1:T(8,128)(2,1)}, bf16[512,2,256]{0,2,1:T(8,128)(2,1)}, u32[]{:S(2)}, u32[]{:S(2)}) collective-permute-start(bf16[512,2,256]{0,2,1:T(8,128)(2,1)} %collective-permute-done.2), channel_id=1, source_target_pairs={{0,1},{1,2},{2,3},{3,4},{4,5},{5,6},{6,7},{7,0},{8,9},{9,10},{10,1... | collective-permute-start | bytes 1572872 | tf_op jit(solution)/shard_map/ppermute | solution.py:25
  266.7 19.7 %copy-start = (bf16[192,2,4096]{2,0,1:T(8,128)(2,1)S(1)}, bf16[192,2,4096]{2,0,1:T(8,128)(2,1)}, u32[]{:S(2)}) copy-start(bf16[192,2,4096]{2,0,1:T(8,128)(2,1)} %all-reduce.4.cloned.1.call-done) | copy-start | bytes 9437188
  269.1 14.6 %copy-start.1 = (bf16[512,2,256]{0,2,1:T(8,128)(2,1)S(1)}, bf16[512,2,256]{0,2,1:T(8,128)(2,1)}, u32[]{:S(2)}) copy-start(bf16[512,2,256]{0,2,1:T(8,128)(2,1)} %get-tuple-element.12) | copy-start | bytes 1572868
  269.1 24.9 %collective-permute-start.6 = (bf16[512,2,256]{0,2,1:T(8,128)(2,1)}, bf16[512,2,256]{0,2,1:T(8,128)(2,1)}, u32[]{:S(2)}, u32[]{:S(2)}) collective-permute-start(bf16[512,2,256]{0,2,1:T(8,128)(2,1)} %collective-permute-done.5), channel_id=1, source_target_pairs={{1,0},{2,1},{3,2},{4,3},{5,4},{6,5},{7,6},{0,7},{9,8},{10,9},{11,1... | collective-permute-start | bytes 1572872 | tf_op jit(solution)/shard_map/ppermute | solution.py:27
  292.0 120.6 %all-reduce.8.cloned.1.call-start = ((), (), s32[]{:S(2)}) async-start(), calls=%async_computation.5 | async-start | bytes 1048576 | tf_op jit(solution)/shard_map/psum | solution.py:69
Sparse Core Ops, SparseCore 0:
  13.1 89.8 all-reduce.3
  109.7 89.5 reduce-scatter.1
  203.1 65.1 all-gather.1
  292.1 61.9 all-reduce.5
  357.5 55.1 all-reduce.7
